TPU v7x, 768 devices: a whole 4x8x12 slice. The times are simulated.
768 devices in a mesh: group: 8 (over y), blk: 32 (over x, z_lo, core), att: 3 (over z_hi).
Axes of the slice: x: 4, y: 8, z: 12 (z_hi: 3, z_lo: 4; z = z_hi * 4 + z_lo), core: 2. Of those that a mesh axis runs over, the one named last changes fastest.
Arguments:
- tokens: bfloat16 [32768, 4096], P(('group', 'blk')), may hold values from -6 to 6
- routed_experts: int32 [32768, 8], P(('group', 'blk')), may hold values from 0 to 127, all different within a row; in each aligned block of 128 rows (0 to 127, 128 to 255, ...) at most 16 rows name the same one
- act_cotangent: bfloat16 [32768, 8, 768], P(('group', 'blk'), None, 'att'), may hold values from -0.625 to 0.625
- weight_codes: bfloat16 [4096, 8, 2, 768], P('blk', 'group', None, 'att'), may hold values from -0.09375 to 0.09375
- weight_scales: bfloat16 [32, 8, 2, 6], P('blk', 'group', None, 'att'), may hold values from 0.3984375 to 2.5
Outputs:
- gate_up_gradient: bfloat16 [4096, 8, 2, 768], P('blk', 'group', None, 'att')
Inputs may be any that keep to these rules, and one draw needn't show every extreme that they name: `routed_experts`: each row names 8 different experts. Among the 128 rows of one device (aligned blocks of 128 rows), no expert is named by more than 16 rows, a bound that some block reaches.
All inputs are finite; a program needn't handle non-finite values.
Results may differ from a plain program's by a relative error of at most 0.023.
Values may be sent and summed in bfloat16 or wider, within the bound.
A program may use at most 64 MiB of HBM per device.

v0:
```python
import jax
import jax.numpy as jnp
from jax import lax
from jax.sharding import PartitionSpec as P

QB = 128
CAP = 16


def in_one_piece(arrays, axis, split_dim, concat_dim, along):
    ends, at = ([], 0)
    for a in arrays[:-1]:
        at += a.shape[along]
        ends.append(at)
    both = jnp.concatenate(arrays, axis=along)
    return tuple(
        jnp.split(
            lax.all_to_all(both, axis, split_axis=split_dim, concat_axis=concat_dim, tiled=True),
            ends,
            axis=along,
        )
    )


def sent_together(arrays, axis, dim, along):
    both = jnp.concatenate(arrays, axis=along)
    filled, at, outs = (lax.all_gather(both, axis, axis=dim, tiled=True), 0, [])
    for a in arrays:
        outs.append(lax.slice_in_dim(filled, at, at + a.shape[along], axis=along))
        at += a.shape[along]
    return tuple(outs)


def swiglu_back(gate_up, cotangent_rows):
    gate_pre = gate_up[:, 0]
    up_pre = gate_up[:, 1]
    sigmoid_gate = jax.nn.sigmoid(gate_pre)
    gate_cotangent = (
        cotangent_rows * up_pre * sigmoid_gate * (1.0 + gate_pre * (1.0 - sigmoid_gate))
    )
    up_cotangent = cotangent_rows * gate_pre * sigmoid_gate
    return jnp.stack([gate_cotangent, up_cotangent], axis=1).astype(jnp.bfloat16)


def local(tokens, routed_experts, act_cotangent, weight_codes, weight_scales):
    groups = lax.axis_size("group")
    hidden_dev = weight_codes.shape[3]
    flight_ids = jnp.arange(groups, dtype=jnp.int32)
    matches = (routed_experts[:, :, None] == flight_ids[None, None, :]).astype(jnp.float32)
    chosen = jnp.sum(matches, axis=1)
    position = jnp.cumsum(chosen, axis=0) - 1.0
    slot_index = jnp.arange(CAP, dtype=jnp.int32).astype(jnp.float32)
    selector = (
        chosen.T[:, None, :]
        * (position.T[:, None, :] == slot_index[None, :, None]).astype(jnp.float32)
    ).astype(jnp.bfloat16)
    sent_tokens = jnp.einsum(
        "ect,td->ecd", selector, tokens, preferred_element_type=jnp.float32
    ).astype(jnp.bfloat16)
    pair_cotangent = jnp.einsum(
        "tke,tkh->teh",
        matches.astype(jnp.bfloat16),
        act_cotangent,
        preferred_element_type=jnp.float32,
    ).astype(jnp.bfloat16)
    sent_cotangent = jnp.einsum(
        "ect,teh->ech", selector, pair_cotangent, preferred_element_type=jnp.float32
    ).astype(jnp.bfloat16)
    arrived_tokens, arrived_cotangent = in_one_piece(
        (sent_tokens, sent_cotangent), "group", 0, 0, 2
    )
    row_count = groups * CAP
    width = arrived_tokens.shape[2]
    token_rows = arrived_tokens.reshape(row_count, width)
    cotangent_rows = arrived_cotangent.reshape(row_count, hidden_dev).astype(jnp.float32)
    local_scales = jnp.repeat(weight_scales, QB, axis=0)
    code_piece, scale_piece = sent_together((weight_codes, local_scales), "blk", 0, 3)
    expanded = jnp.repeat(scale_piece[:, 0].astype(jnp.float32), QB, axis=2)
    weights = (code_piece[:, 0].astype(jnp.float32) * expanded).astype(jnp.bfloat16)
    gate_up = jnp.einsum("rn,njh->rjh", token_rows, weights, preferred_element_type=jnp.float32)
    pre_cotangent = swiglu_back(gate_up, cotangent_rows)
    own_columns = lax.all_to_all(token_rows, "blk", split_axis=1, concat_axis=0, tiled=True)
    piece = lax.all_gather(pre_cotangent, "blk", axis=0, tiled=True)
    shards = piece.shape[0] // row_count
    column_block = own_columns
    column_block = column_block.reshape(shards, row_count, column_block.shape[1])
    cotangent_block = piece.reshape(shards, row_count, 2, hidden_dev)
    partials = jnp.einsum(
        "krd,krjh->kdjh", column_block, cotangent_block, preferred_element_type=jnp.float32
    )
    rounded = lax.optimization_barrier(partials.astype(jnp.bfloat16)).astype(jnp.float32)
    gradient = jnp.sum(rounded, axis=0)
    return gradient.astype(jnp.bfloat16)[:, None]


def solution(mesh):
    return jax.shard_map(
        local,
        mesh=mesh,
        in_specs=(
            P(("group", "blk"), None),
            P(("group", "blk"), None),
            P(("group", "blk"), None, "att"),
            P("blk", "group", None, "att"),
            P("blk", "group", None, "att"),
        ),
        out_specs=P("blk", "group", None, "att"),
        check_vma=False,
    )
```

profile of v0, /device:TPU:1, one launch (start us, length us, event | category | flops | bytes accessed | tf_op | source)
XLA Modules:
  0.0 190.0 jit_solution(6917843044699912201)
XLA Ops:
  6.5 1.1 copy.25
  7.7 0.7 reshape.57
  8.4 0.7 pad_maximum_fusion.1
  9.2 0.7 convert_reduce_fusion
  10.0 0.2 reduce_window_sum.11
  10.2 0.7 convert_convert_fusion
  10.9 0.2 copy.22
  11.1 1.3 convolution_convert_fusion.1
  12.5 0.2 convolution_convert_fusion.2
  12.7 0.5 convolution_convert_fusion
  13.3 31.6 %all_to_all.21 = bf16[8,16,4352]{2,1,0:T(8,128)(2,1)S(1)} all-to-all(bf16[8,16,4352]{2,1,0:T(8,128)(2,1)S(1)} %pad_maximum_fusion), channel_id=1, replica_groups=mesh['group'=8,'blk'=32,'att'=3] {'group'}, dimensions={0} | all-to-all | bytes 2228224 | tf_op jit(solution)/shard_map/all_to_all | solution.py:18
  45.0 49.2 %all-gather.3.cloned.1.call-done = bf16[4096,1,2,258]{0,3,2,1:T(8,128)(2,1)} async-done(((bf16[128,1,2,258]{0,3,2,1:T(8,128)(2,1)}), bf16[4096,1,2,258]{0,3,2,1:T(8,128)(2,1)}) %all-gather.3.cloned.1.call-update) | async-done | bytes 4227088 | tf_op jit(solution)/shard_map/all_gather | solution.py:27
  94.2 0.9 fusion.14
  95.2 2.2 %slice-done = bf16[4096,1,2,256]{0,3,2,1:T(8,128)(2,1)S(1)} async-done(((bf16[4096,1,2,258]{0,3,2,1:T(8,128)(2,1)}), bf16[4096,1,2,256]{0,3,2,1:T(8,128)(2,1)S(1)}, s32[]{:S(2)}) %slice-start) | async-done | bytes 4194328 | tf_op jit(solution)/shard_map/slice | solution.py:29
  97.3 1.1 fusion
  98.5 1.5 fusion.25
  100.1 0.7 pad_maximum_fusion.2
  100.8 0.2 copy.31
  101.0 1.7 copy.24
  102.8 39.1 %all_to_all.22 = bf16[128,32,128]{0,2,1:T(8,128)(2,1)S(1)} all-to-all(bf16[128,32,128]{0,2,1:T(8,128)(2,1)} %copy.24), channel_id=1, replica_groups=mesh['group'=8,'blk'=32,'att'=3] {'blk'}, dimensions={1} | all-to-all | bytes 2097152 | tf_op jit(solution)/shard_map/all_to_all | solution.py:82
  141.9 32.2 %all-gather.5.cloned.1.call-done = bf16[4096,2,256]{2,0,1:T(8,128)(2,1)} async-done(((bf16[128,2,256]{2,0,1:T(8,128)(2,1)}), bf16[4096,2,256]{2,0,1:T(8,128)(2,1)}) %all-gather.5.cloned.1.call-update) | async-done | bytes 4194320 | tf_op jit(solution)/shard_map/all_gather | solution.py:83
  174.1 5.4 %fusion.3 = bf16[32,128,2,256]{3,1,2,0:T(8,128)(2,1)} fusion(bf16[32,128,2,256]{3,1,0,2:T(8,128)(2,1)} %bitcast.42, bf16[128,32,128]{0,2,1:T(8,128)(2,1)S(1)} %all_to_all.22), kind=kOutput, calls=%fused_computation.5 | convolution fusion | flops 538968064 | bytes 9437184 | tf_op jit(solution)/shard_map/krd,krjh->kdjh/dot_general | solution.py:88
  179.5 2.8 %reduce_sum.22 = bf16[128,2,256]{2,0,1:T(8,128)(2,1)S(1)} reduce(bf16[32,128,2,256]{3,1,2,0:T(8,128)(2,1)} %fusion.3, bf16[]{:T(256)} %constant.12.clone.1), dimensions={0}, to_apply=%region_2.3 | reduce | flops 2031616 | bytes 4325378 | tf_op jit(solution)/shard_map/reduce_sum | solution.py:92
  182.3 0.8 copy.28
  (18 shorter events, 0.5 us)
Async XLA Ops:
  6.5 6.2 %copy-start = (bf16[128,4096]{1,0:T(8,128)(2,1)S(1)}, bf16[128,4096]{1,0:T(8,128)(2,1)}, u32[]{:S(2)}) copy-start(bf16[128,4096]{1,0:T(8,128)(2,1)} %param.5) | copy-start | bytes 3145732
  6.5 87.7 %all-gather.3.cloned.1.call-start = ((), (), s32[]{:S(2)}) async-start(), calls=%async_computation.2 | async-start | bytes 4460544 | tf_op jit(solution)/shard_map/all_gather | solution.py:27
  9.1 165.0 %all-gather.5.cloned.1.call-start = ((), (), s32[]{:S(2)}) async-start(), calls=%async_computation.3 | async-start | bytes 4325376 | tf_op jit(solution)/shard_map/all_gather | solution.py:83
  44.9 50.3 %copy-start.1 = (bf16[8,16,4352]{2,1,0:T(8,128)(2,1)}, bf16[8,16,4352]{2,1,0:T(8,128)(2,1)S(1)}, u32[]{:S(2)}) copy-start(bf16[8,16,4352]{2,1,0:T(8,128)(2,1)S(1)} %all_to_all.21) | copy-start | bytes 3342340
  95.2 2.2 %slice-start = ((bf16[4096,1,2,258]{0,3,2,1:T(8,128)(2,1)}), bf16[4096,1,2,256]{0,3,2,1:T(8,128)(2,1)S(1)}, s32[]{:S(2)}) async-start(bf16[4096,1,2,258]{0,3,2,1:T(8,128)(2,1)} %all-gather.3.cloned.1.call-done), calls=%async_computation.4 | async-start | bytes 8388608 | tf_op jit(solution)/shard_map/slice | solution.py:29
  98.5 1.5 slice-start.1
Sparse Core Ops, SparseCore 0:
  9.7 84.5 all-gather.2
  100.9 73.1 all-gather.4
where the time goes:
time: 190 us
  waiting for transfers between devices  81.5 us (43%)
  blocking collectives  70.8 us (37%)
  between operations  13.5 us (7%)
  matrix products  8.95 us (5%)
  other arithmetic  7.97 us (4%)
  local copies, waits for them, and re-layouts  7.23 us (4%)
    all_gather x1, waiting for transfers between devices, sent_together(): filled, at, outs = (lax.all_gather(both, axis, axis=dim, tiled=True), 0, [])  49.2 us
    all_to_all x1, blocking collectives, local(): lax.all_to_all(token_rows, 'blk', split_axis=1, concat_axis=0, tiled=True)  39.1 us
    all_gather x1, waiting for transfers between devices, local(): piece = lax.all_gather(pre_cotangent, 'blk', axis=0, tiled=True)  32.2 us
    all_to_all x1, blocking collectives, in_one_piece(): lax.all_to_all(both, axis, split_axis=split_dim, concat_axis=concat_dim,...  31.6 us
    dot_general x1, matrix products, local(): jnp.einsum('krd,krjh->kdjh', column_block, cotangent_block, preferred_ele...  5.39 us
  transfers between devices with their start and end apart: 2, of which 2 were waited for; matrix products, arithmetic and copies ran while one was open for 3% of the time, Pallas kernels for 0%

commit v1 on v0

v1 whole, which is shorter than its diff:
```python
import functools

import jax
import jax.numpy as jnp
from jax import lax
from jax.experimental import pallas as pl
from jax.experimental.pallas import tpu as pltpu
from jax.sharding import PartitionSpec as P

MESH = pl.DeviceIdType.MESH
CAP = 16
NY, NX, NZ, NC = 8, 4, 4, 2
BF = jnp.bfloat16
F32 = jnp.float32


def dot(a, b):
    return jnp.dot(a, b, preferred_element_type=F32)


def kernel(
    tokens_hbm, routed_hbm, act_hbm, codes_hbm, scales_hbm, out_ref,
    tok, routed, act, codes, scales, codes32, spread, send, recv, relay,
    w, part, other, cot_other, p_t, g, r_a, r_b, f_l, f_r, z_buf,
    in_sem, own_sem, a_send, a_recv, rl_send, rl_recv,
    wz_send, wz_recv, wx_send, wx_recv, ex_send, ex_recv,
    rs_send, rs_recv, z_send, z_recv,
):
    y = lax.axis_index("group")
    b = lax.axis_index("blk")
    x, z, c = b // (NZ * NC), (b // NC) % NZ, b % NC
    half = send.shape[3] - 128
    hid = act.shape[1]

    def blk_of(xx, zz, cc):
        return xx * (NZ * NC) + zz * NC + cc

    right, left, across = (x + 1) % NX, (x + NX - 1) % NX, (x + 2) % NX
    to_right = {"blk": blk_of(right, z, c)}
    to_left = {"blk": blk_of(left, z, c)}
    partner = {"blk": blk_of(x, z, 1 - c)}

    def remote(src, dst, s_sem, r_sem, where):
        return pltpu.make_async_remote_copy(
            src_ref=src, dst_ref=dst, send_sem=s_sem, recv_sem=r_sem,
            device_id=where, device_id_type=MESH,
        )

    loads = [
        pltpu.make_async_copy(codes_hbm, codes, in_sem.at[0]),
        pltpu.make_async_copy(scales_hbm, scales, in_sem.at[1]),
        pltpu.make_async_copy(routed_hbm, routed, in_sem.at[2]),
        pltpu.make_async_copy(tokens_hbm, tok, in_sem.at[3]),
        pltpu.make_async_copy(act_hbm, act, in_sem.at[4]),
    ]
    for load in loads:
        load.start()

    barrier = pltpu.get_barrier_semaphore()
    greeted = 0
    for dy in (1, 2, 3, 5, 6, 7):
        for cc in range(NC):
            pl.semaphore_signal(
                barrier, inc=1,
                device_id={"group": (y + dy) % NY, "blk": blk_of(x, z, cc)},
                device_id_type=MESH,
            )
            greeted += 1
    for where in [partner, to_right, to_left] + [
        {"blk": blk_of(x, (z + k) % NZ, c)} for k in range(1, NZ)
    ]:
        pl.semaphore_signal(barrier, inc=1, device_id=where, device_id_type=MESH)
        greeted += 1

    loads[0].wait()
    loads[1].wait()
    codes32[...] = codes[:, 0].astype(F32)
    sc = scales[0, 0].astype(F32)
    mine_w = z * NX + x
    for j in range(2):
        for q in range(hid // 128):
            piece = codes32[:, j, q * 128:(q + 1) * 128] * sc[j:j + 1, q:q + 1]
            at = q * 256 + j * 128
            w[mine_w, :, at:at + 128] = piece.astype(BF)

    loads[2].wait()
    ids = routed[...]
    lane = lax.broadcasted_iota(jnp.int32, (128, 128), 1)
    row = lax.broadcasted_iota(jnp.int32, (128, 128), 0)
    expert_of, slot_of = lane // CAP, lane % CAP
    hits = [
        jnp.where(ids[:, k:k + 1] == expert_of, 1.0, 0.0) for k in range(ids.shape[1])
    ]
    chosen = functools.reduce(lambda p, q: p + q, hits)
    before = jnp.where(lane < row, 1.0, 0.0).astype(BF)
    position = dot(before, chosen.astype(BF))
    select = jnp.where(position == slot_of.astype(F32), chosen, 0.0)
    for k in range(len(hits)):
        spread[:, k, :] = select * hits[k]
    select_t = select.T.astype(BF)
    pick = spread[...].reshape(128 * len(hits), 128).astype(BF)
    loads[4].wait()
    cot = lax.dot_general(pick, act[...], (((0,), (0,)), ((), ())), preferred_element_type=F32)
    for j in range(NC):
        send[:, j, :, half:half + 128] = (
            cot[:, j * 128:(j + 1) * 128].astype(BF).reshape(NY, CAP, 128)
        )

    pl.semaphore_wait(barrier, greeted)

    wz = []
    for k in range(1, NZ):
        cp = remote(
            w.at[mine_w], w.at[mine_w], wz_send.at[k], wz_recv.at[k],
            {"blk": blk_of(x, (z + k) % NZ, c)},
        )
        cp.start()
        wz.append(cp)

    def wx_copies(k):
        zz = (z + NZ - k) % NZ
        at = zz * NX + x
        return [
            remote(w.at[at], w.at[at], wx_send.at[0, k], wx_recv.at[0, k], to_right),
            remote(w.at[at], w.at[at], wx_send.at[1, k], wx_recv.at[1, k], to_left),
        ]

    def wx_relays(k):
        zz = (z + NZ - k) % NZ
        from_l, from_r = zz * NX + left, zz * NX + right
        top, low = pl.ds(0, 64), pl.ds(64, 64)
        return [
            remote(w.at[from_l, top], w.at[from_l, top], wx_send.at[2, k], wx_recv.at[2, k], to_right),
            remote(w.at[from_r, low], w.at[from_r, low], wx_send.at[3, k], wx_recv.at[3, k], to_left),
        ]

    wx = [wx_copies(k) for k in range(NZ)]
    wr = [wx_relays(k) for k in range(NZ)]
    for cp in wx[0]:
        cp.start()

    loads[3].wait()
    for pair in range(NX * NZ):
        rows = dot(select_t, tok[:, pair * 256:(pair + 1) * 256]).astype(BF)
        at = ((pair % NZ) * NX + pair // NZ) * 128
        for j in range(NC):
            send[:, j, :, at:at + 128] = rows[:, j * 128:(j + 1) * 128].reshape(NY, CAP, 128)

    here = y * NC + c
    first_legs = [
        remote(
            send.at[(y + 4) % NY, j], relay.at[j], rl_send.at[j], rl_recv.at[j],
            {"group": (y + (2 if j == 0 else NY - 2)) % NY},
        )
        for j in range(NC)
    ]
    for cp in first_legs:
        cp.start()
    direct = []
    for n, dy in enumerate((3, 5, 2, 6, 1, 7)):
        to = (y + dy) % NY
        for j in range(NC):
            cp = remote(
                send.at[to, j], recv.at[here], a_send.at[n * NC + j], a_recv.at[here],
                {"group": to, "blk": blk_of(x, z, j)},
            )
            cp.start()
            direct.append(cp)
    own = pltpu.make_async_copy(send.at[y, c], recv.at[here], own_sem)
    own.start()
    cross = remote(send.at[y, 1 - c], recv.at[here], a_send.at[12], a_recv.at[here], partner)
    cross.start()

    for k in range(1, NZ):
        wz[k - 1].wait_recv()
        for cp in wx[k]:
            cp.start()
    second_legs = []
    for j in range(NC):
        first_legs[j].wait_recv()
        source = (y + (NY - 2 if j == 0 else 2)) % NY
        to = (y + (2 if j == 0 else NY - 2)) % NY
        slot = source * NC + c
        cp = remote(
            relay.at[j], recv.at[slot], a_send.at[13 + j], a_recv.at[slot],
            {"group": to, "blk": blk_of(x, z, j)},
        )
        cp.start()
        second_legs.append(cp)
    for k in range(NZ):
        for cp, onward in zip(wx[k], wr[k]):
            cp.wait_recv()
            onward.start()
    for k in range(NZ):
        for cp in wr[k]:
            cp.wait_recv()
    own.wait()
    for n in range(1, NY * NC):
        slot = (here + n) % (NY * NC)
        remote(
            recv.at[slot], recv.at[slot], a_send.at[15], a_recv.at[slot], partner
        ).wait_recv()

    swap_cot = remote(
        recv.at[:, :, pl.ds(half, 128)], cot_other, ex_send.at[2], ex_recv.at[2], partner
    )
    swap_cot.start()
    swaps = []
    rows_here = recv[:, :, :half].reshape(NY * NC * CAP, half)
    for q in range(hid // 128):
        part[q] = dot(rows_here, w[:, :, q * 256:(q + 1) * 256].reshape(half, 256))
        cp = remote(part.at[q], other.at[q], ex_send.at[q], ex_recv.at[q], partner)
        cp.start()
        swaps.append(cp)
    swap_cot.wait_recv()
    for q in range(hid // 128):
        swaps[q].wait_recv()
        gate = part[q, :, :128] + other[q, :, :128]
        up = part[q, :, 128:] + other[q, :, 128:]
        mine = recv[:, :, half:].reshape(NY * NC * CAP, 128).astype(F32)
        theirs = cot_other[...].reshape(NY * NC * CAP, 128).astype(F32)
        cotangent = jnp.where(c == q, mine, theirs)
        s = jax.nn.sigmoid(gate)
        d_gate = cotangent * up * s * (1.0 + gate * (1.0 - s))
        d_up = cotangent * gate * s
        p_t[q * 128:(q + 1) * 128, :] = d_gate.T.astype(BF)
        p_t[hid + q * 128:hid + (q + 1) * 128, :] = d_up.T.astype(BF)

    upper, lower = pl.ds(0, hid), pl.ds(hid, hid)

    def z_of(k):
        return (z + 1 + k) % NZ

    def product(k):
        zz = z_of(k)
        cols = recv[:, :, pl.ds(pl.multiple_of(zz * (NX * 128), 128), NX * 128)].reshape(
            NY * NC * CAP, NX * 128
        )
        for m in range(2):
            got = dot(p_t[m * hid:(m + 1) * hid, :], cols).astype(BF)
            for xx in range(NX):
                g[zz, xx, m * hid:(m + 1) * hid, :] = got[:, xx * 128:(xx + 1) * 128]

    def sends(k):
        zz = z_of(k)
        return [
            remote(g.at[zz, across, upper], r_a.at[zz], rs_send.at[0, k], rs_recv.at[0, k], to_right),
            remote(g.at[zz, across, lower], r_b.at[zz], rs_send.at[1, k], rs_recv.at[1, k], to_left),
            remote(g.at[zz, right, lower], f_l.at[zz, lower], rs_send.at[2, k], rs_recv.at[2, k], to_right),
            remote(g.at[zz, left, upper], f_r.at[zz, upper], rs_send.at[3, k], rs_recv.at[3, k], to_left),
            remote(g.at[zz, right, upper], f_l.at[zz, upper], rs_send.at[4, k], rs_recv.at[4, k], to_right),
            remote(g.at[zz, left, lower], f_r.at[zz, lower], rs_send.at[5, k], rs_recv.at[5, k], to_left),
        ]

    rs = [sends(k) for k in range(NZ)]
    zs = [
        remote(
            g.at[z_of(k), x], z_buf.at[k], z_send.at[k], z_recv.at[k],
            {"blk": blk_of(x, z_of(k), c)},
        )
        for k in range(NZ - 1)
    ]

    def begin(k):
        product(k)
        for cp in rs[k][:4]:
            cp.start()

    def pass_on(k):
        zz = z_of(k)
        rs[k][0].wait_recv()
        g[zz, right, upper] = (g[zz, right, upper].astype(F32) + r_a[zz].astype(F32)).astype(BF)
        rs[k][4].start()
        rs[k][1].wait_recv()
        g[zz, left, lower] = (g[zz, left, lower].astype(F32) + r_b[zz].astype(F32)).astype(BF)
        rs[k][5].start()

    def gathered(k):
        zz = z_of(k)
        for cp in rs[k][2:]:
            cp.wait_recv()
        return g[zz, x].astype(F32) + f_l[zz].astype(F32) + f_r[zz].astype(F32)

    def finish(k):
        g[z_of(k), x] = gathered(k).astype(BF)
        zs[k].start()

    begin(0)
    begin(1)
    for k in range(NZ):
        pass_on(k)
        if k + 2 < NZ:
            begin(k + 2)
        if k >= 1:
            finish(k - 1)
    total = gathered(NZ - 1)
    for k in range(NZ - 1):
        zs[k].wait_recv()
        total = total + z_buf[k].astype(F32)
    out_ref[...] = total.T.astype(BF)

    for cp in wz + direct + first_legs + second_legs + swaps + zs + [swap_cot, cross]:
        cp.wait_send()
    for group in wx + wr + rs:
        for cp in group:
            cp.wait_send()


def local(tokens, routed_experts, act_cotangent, weight_codes, weight_scales):
    rows, width = tokens.shape
    top, hid = act_cotangent.shape[1:]
    half = width // 2
    dma = pltpu.SemaphoreType.DMA
    any_spec = pl.BlockSpec(memory_space=pl.ANY)
    out = pl.pallas_call(
        kernel,
        out_shape=jax.ShapeDtypeStruct((rows, 2 * hid), BF),
        in_specs=[any_spec] * 5,
        out_specs=pl.BlockSpec(memory_space=pltpu.VMEM),
        scratch_shapes=[
            pltpu.VMEM((rows, width), BF),
            pltpu.VMEM((rows, top), jnp.int32),
            pltpu.VMEM((rows * top, hid), BF),
            pltpu.VMEM((rows, 1, 2, hid), BF),
            pltpu.VMEM((1, 1, 2, hid // 128), BF),
            pltpu.VMEM((rows, 2, hid), F32),
            pltpu.VMEM((rows, top, 128), F32),
            pltpu.VMEM((NY, NC, CAP, half + 128), BF),
            pltpu.VMEM((NY * NC, CAP, half + 128), BF),
            pltpu.VMEM((NC, CAP, half + 128), BF),
            pltpu.VMEM((NX * NZ, 128, 2 * hid), BF),
            pltpu.VMEM((2, NY * NC * CAP, hid), F32),
            pltpu.VMEM((2, NY * NC * CAP, hid), F32),
            pltpu.VMEM((NY * NC, CAP, 128), BF),
            pltpu.VMEM((2 * hid, NY * NC * CAP), BF),
            pltpu.VMEM((NZ, NX, 2 * hid, 128), BF),
            pltpu.VMEM((NZ, hid, 128), BF),
            pltpu.VMEM((NZ, hid, 128), BF),
            pltpu.VMEM((NZ, 2 * hid, 128), BF),
            pltpu.VMEM((NZ, 2 * hid, 128), BF),
            pltpu.VMEM((NZ, 2 * hid, 128), BF),
            dma((5,)), dma,
            dma((16,)), dma((16,)), dma((2,)), dma((2,)),
            dma((NZ,)), dma((NZ,)), dma((4, NZ)), dma((4, NZ)),
            dma((3,)), dma((3,)),
            dma((6, NZ)), dma((6, NZ)), dma((NZ,)), dma((NZ,)),
        ],
        compiler_params=pltpu.CompilerParams(
            collective_id=0, has_side_effects=True, vmem_limit_bytes=48 * 1024 * 1024
        ),
    )(tokens, routed_experts, act_cotangent.reshape(rows * top, hid), weight_codes, weight_scales)
    return out.reshape(rows, 1, 2, hid)


def solution(mesh):
    return jax.shard_map(
        local,
        mesh=mesh,
        in_specs=(
            P(("group", "blk"), None),
            P(("group", "blk"), None),
            P(("group", "blk"), None, "att"),
            P("blk", "group", None, "att"),
            P("blk", "group", None, "att"),
        ),
        out_specs=P("blk", "group", None, "att"),
        check_vma=False,
    )
```

time: 190 us -> 70.5 us (0.37)
  waiting for transfers between devices: 81.5 us -> 0 us
  blocking collectives: 70.8 us -> 0 us
  Pallas kernels: 0 us -> 65.6 us
  between operations: 13.5 us -> 0.02 us
  matrix products: 8.95 us -> 0 us
  other arithmetic: 7.97 us -> 0 us
  local copies, waits for them, and re-layouts: 7.23 us -> 4.66 us
    all_gather x2 -> x0, waiting for transfers between devices: 81.4 us -> none  [the longest x1 49.2 us: sent_together(): filled, at, outs = (lax.all_gather(both, axis, axis=dim, tiled=True), 0, [])]
    all_to_all x2 -> x0, blocking collectives: 70.8 us -> none  [the longest x1 39.1 us: local(): lax.all_to_all(token_rows, 'blk', split_axis=1, concat_axis=0, tiled=True)]
    pallas_call x0 -> x1, Pallas kernels: none -> 65.6 us  [local(): pl.pallas_call(kernel, out_shape=jax.ShapeDtypeStruct((rows, 2 * hid), BF...]
    dot_general x5 -> x0, matrix products: 8.95 us -> none  [the longest x1 5.39 us: local(): jnp.einsum('krd,krjh->kdjh', column_block, cotangent_block, preferred_ele...]
    reduce_sum x2 -> x0, other arithmetic: 3.54 us -> none  [the longest x1 2.84 us: local(): gradient = jnp.sum(rounded, axis=0)]
    convert_element_type x4 -> x0, other arithmetic: 2.74 us -> none  [the longest x1 1.1 us: local(): (code_piece[:, 0].astype(jnp.float32) * expanded).astype(jnp.bfloat16)]
    unnamed x6 -> x9, local copies, waits for them, and re-layouts: 1.37 us -> 3.97 us
    slice x2 -> x0, local copies, waits for them, and re-layouts: 2.17 us -> none  [sent_together(): outs.append(lax.slice_in_dim(filled, at, at + a.shape[along], axis=along))]
  transfers between devices with their start and end apart: 2 -> 0, of which waited for: 2 -> 0; matrix products, arithmetic and copies ran while one was open for 3% -> 0% of each run, Pallas kernels for 0% -> 0%
where the time goes in v1:
time: 70.5 us; the launch traced here: 70.3 us
  Pallas kernels  65.6 us (93%)
  local copies, waits for them, and re-layouts  4.66 us (7%)
    pallas_call x1, Pallas kernels, local(): pl.pallas_call(kernel, out_shape=jax.ShapeDtypeStruct((rows, 2 * hid), BF...  65.6 us
    unnamed x9, local copies, waits for them, and re-layouts  3.97 us

profile of v1, /device:TPU:1, one launch (start us, length us, event | category | flops | bytes accessed | tf_op | source)
XLA Modules:
  0.0 70.3 jit_solution(48535705721297911)
XLA Ops:
  0.0 0.0 copy-start.3
  0.0 0.8 %copy.6.routed_hbm = s32[128,8]{1,0:T(8,128)S(1)} copy(s32[128,8]{0,1:T(8,128)} %param.6) | data formatting | bytes 8192 | tf_op args[1]
  0.8 0.0 copy-done.3
  0.8 0.0 copy-start
  0.8 1.2 %copy-done = bf16[128,4096]{1,0:T(8,128)(2,1)S(1)} copy-done((bf16[128,4096]{1,0:T(8,128)(2,1)S(1)}, bf16[128,4096]{1,0:T(8,128)(2,1)}, u32[]{:S(2)}) %copy-start) | copy-done | bytes 1048600
  2.0 0.0 copy-start.1
  2.0 1.0 %copy-done.1 = bf16[128,8,256]{2,1,0:T(8,128)(2,1)S(1)} copy-done((bf16[128,8,256]{2,1,0:T(8,128)(2,1)S(1)}, bf16[128,8,256]{2,1,0:T(8,128)(2,1)}, u32[]{:S(2)}) %copy-start.1) | copy-done | bytes 524312
  3.1 0.0 copy-start.2
  3.1 0.9 %copy-done.2 = bf16[128,1,2,256]{3,2,1,0:T(2,128)(2,1)S(1)} copy-done((bf16[128,1,2,256]{3,2,1,0:T(2,128)(2,1)S(1)}, bf16[128,1,2,256]{3,2,1,0:T(2,128)(2,1)}, u32[]{:S(2)}) %copy-start.2) | copy-done | bytes 131096
  4.0 65.6 %shard_map.55 = bf16[128,512]{1,0:T(8,128)(2,1)S(1)} custom-call(bf16[128,4096]{1,0:T(8,128)(2,1)S(1)} %copy-done, s32[128,8]{1,0:T(8,128)S(1)} %copy.6.routed_hbm, bf16[1024,256]{1,0:T(8,128)(2,1)S(1)} %bitcast.2, bf16[128,1,2,256]{3,2,1,0:T(2,128)(2,1)S(1)} %copy-done.2, bf16[1,1,2,2]{3,2,1,0:T(2,128)(2,1)S(1)} %copy-done.3), custom_call_target="tpu_custom_call" | custom-call | tf_op jit(solution)/shard_map/pallas_call | solution.py:315
  69.6 0.7 reshape.7
Async XLA Ops:
  0.0 0.8 %copy-start.3 = (bf16[1,1,2,2]{3,2,1,0:T(2,128)(2,1)S(1)}, bf16[1,1,2,2]{3,2,1,0:T(2,128)(2,1)}, u32[]{:S(2)}) copy-start(bf16[1,1,2,2]{3,2,1,0:T(2,128)(2,1)} %scales_hbm.1) | copy-start | bytes 28
  0.8 1.2 %copy-start = (bf16[128,4096]{1,0:T(8,128)(2,1)S(1)}, bf16[128,4096]{1,0:T(8,128)(2,1)}, u32[]{:S(2)}) copy-start(bf16[128,4096]{1,0:T(8,128)(2,1)} %tokens_hbm.1) | copy-start | bytes 3145732
  2.0 1.0 %copy-start.1 = (bf16[128,8,256]{2,1,0:T(8,128)(2,1)S(1)}, bf16[128,8,256]{2,1,0:T(8,128)(2,1)}, u32[]{:S(2)}) copy-start(bf16[128,8,256]{2,1,0:T(8,128)(2,1)} %param.7) | copy-start | bytes 1572868
  3.1 0.9 %copy-start.2 = (bf16[128,1,2,256]{3,2,1,0:T(2,128)(2,1)S(1)}, bf16[128,1,2,256]{3,2,1,0:T(2,128)(2,1)}, u32[]{:S(2)}) copy-start(bf16[128,1,2,256]{3,2,1,0:T(2,128)(2,1)} %codes_hbm.1) | copy-start | bytes 393220

commit v2 on v1

--- a/solution.py
+++ b/solution.py
@@ -22,7 +22,7 @@
     tokens_hbm, routed_hbm, act_hbm, codes_hbm, scales_hbm, out_ref,
     tok, routed, act, codes, scales, codes32, spread, send, recv, relay,
     w, part, other, cot_other, p_t, g, r_a, r_b, f_l, f_r, z_buf,
-    in_sem, own_sem, a_send, a_recv, rl_send, rl_recv,
+    in_sem, own_sem, ready, a_send, a_recv, rl_send, rl_recv,
     wz_send, wz_recv, wx_send, wx_recv, ex_send, ex_recv,
     rs_send, rs_recv, z_send, z_recv,
 ):
@@ -56,21 +56,25 @@
     for load in loads:
         load.start()
 
+    peers = [(dy, x, z, cc) for dy in (1, 2, 3, 5, 6, 7) for cc in range(NC)]
+    peers += [(0, x, z, 1 - c), (0, right, z, c), (0, left, z, c)]
+    peers += [(0, x, (z + k) % NZ, c) for k in range(1, NZ)]
+
+    def is_last(dy, xx, zz, cc):
+        return ((y + dy) % NY == 0) & (blk_of(xx, zz, cc) == 0)
+
+    def place(dy, xx, zz, cc):
+        return {"group": (y + dy) % NY, "blk": blk_of(xx, zz, cc)}
+
+    last = (y == 0) & (b == 0)
+    by_last = functools.reduce(lambda p, q: p | q, [is_last(*peer) for peer in peers])
+    owed = by_last.astype(jnp.int32)
     barrier = pltpu.get_barrier_semaphore()
-    greeted = 0
-    for dy in (1, 2, 3, 5, 6, 7):
-        for cc in range(NC):
-            pl.semaphore_signal(
-                barrier, inc=1,
-                device_id={"group": (y + dy) % NY, "blk": blk_of(x, z, cc)},
-                device_id_type=MESH,
-            )
-            greeted += 1
-    for where in [partner, to_right, to_left] + [
-        {"blk": blk_of(x, (z + k) % NZ, c)} for k in range(1, NZ)
-    ]:
-        pl.semaphore_signal(barrier, inc=1, device_id=where, device_id_type=MESH)
-        greeted += 1
+
+    @pl.when(jnp.logical_not(last))
+    def _():
+        for peer in peers:
+            pl.semaphore_signal(barrier, inc=1, device_id=place(*peer), device_id_type=MESH)
 
     loads[0].wait()
     loads[1].wait()
@@ -84,7 +88,7 @@
             w[mine_w, :, at:at + 128] = piece.astype(BF)
 
     loads[2].wait()
-    ids = routed[...]
+    ids = routed[...].T
     lane = lax.broadcasted_iota(jnp.int32, (128, 128), 1)
     row = lax.broadcasted_iota(jnp.int32, (128, 128), 0)
     expert_of, slot_of = lane // CAP, lane % CAP
@@ -106,38 +110,47 @@
             cot[:, j * 128:(j + 1) * 128].astype(BF).reshape(NY, CAP, 128)
         )
 
-    pl.semaphore_wait(barrier, greeted)
-
-    wz = []
+    pl.semaphore_wait(barrier, len(peers) - owed)
+
+    @pl.when(last)
+    def _():
+        for peer in peers:
+            pl.semaphore_signal(ready, inc=1, device_id=place(*peer), device_id_type=MESH)
+
+    later = []
+
+    def do(waits, starts, touches_last):
+        def act():
+            for cp in waits:
+                cp.wait_recv()
+            for cp in starts:
+                cp.start()
+
+        pl.when(jnp.logical_not(touches_last))(act)
+        later.append((touches_last, act))
+
+    wz, wx, wr = [None], [], []
     for k in range(1, NZ):
-        cp = remote(
+        wz.append(remote(
             w.at[mine_w], w.at[mine_w], wz_send.at[k], wz_recv.at[k],
             {"blk": blk_of(x, (z + k) % NZ, c)},
-        )
-        cp.start()
-        wz.append(cp)
-
-    def wx_copies(k):
-        zz = (z + NZ - k) % NZ
-        at = zz * NX + x
-        return [
-            remote(w.at[at], w.at[at], wx_send.at[0, k], wx_recv.at[0, k], to_right),
-            remote(w.at[at], w.at[at], wx_send.at[1, k], wx_recv.at[1, k], to_left),
-        ]
-
-    def wx_relays(k):
-        zz = (z + NZ - k) % NZ
-        from_l, from_r = zz * NX + left, zz * NX + right
-        top, low = pl.ds(0, 64), pl.ds(64, 64)
-        return [
-            remote(w.at[from_l, top], w.at[from_l, top], wx_send.at[2, k], wx_recv.at[2, k], to_right),
-            remote(w.at[from_r, low], w.at[from_r, low], wx_send.at[3, k], wx_recv.at[3, k], to_left),
-        ]
-
-    wx = [wx_copies(k) for k in range(NZ)]
-    wr = [wx_relays(k) for k in range(NZ)]
-    for cp in wx[0]:
-        cp.start()
+        ))
+        do([], [wz[k]], is_last(0, x, (z + k) % NZ, c))
+    top, low = pl.ds(0, 64), pl.ds(64, 64)
+    for k in range(NZ):
+        row_of = ((z + NZ - k) % NZ) * NX
+        here_w, left_w, right_w = w.at[row_of + x], w.at[row_of + left], w.at[row_of + right]
+        wx.append([
+            remote(here_w, here_w, wx_send.at[0, k], wx_recv.at[0, k], to_right),
+            remote(here_w, here_w, wx_send.at[1, k], wx_recv.at[1, k], to_left),
+        ])
+        wr.append([
+            remote(left_w.at[top], left_w.at[top], wx_send.at[2, k], wx_recv.at[2, k], to_right),
+            remote(right_w.at[low], right_w.at[low], wx_send.at[3, k], wx_recv.at[3, k], to_left),
+        ])
+    right_last, left_last = is_last(0, right, z, c), is_last(0, left, z, c)
+    do([], [wx[0][0]], right_last)
+    do([], [wx[0][1]], left_last)
 
     loads[3].wait()
     for pair in range(NX * NZ):
@@ -147,50 +160,58 @@
             send[:, j, :, at:at + 128] = rows[:, j * 128:(j + 1) * 128].reshape(NY, CAP, 128)
 
     here = y * NC + c
-    first_legs = [
-        remote(
+    first_legs, second_legs, direct = [], [], []
+    for j in range(NC):
+        dy = 2 if j == 0 else NY - 2
+        cp = remote(
             send.at[(y + 4) % NY, j], relay.at[j], rl_send.at[j], rl_recv.at[j],
-            {"group": (y + (2 if j == 0 else NY - 2)) % NY},
-        )
-        for j in range(NC)
-    ]
-    for cp in first_legs:
-        cp.start()
-    direct = []
-    for n, dy in enumerate((3, 5, 2, 6, 1, 7)):
-        to = (y + dy) % NY
-        for j in range(NC):
-            cp = remote(
-                send.at[to, j], recv.at[here], a_send.at[n * NC + j], a_recv.at[here],
-                {"group": to, "blk": blk_of(x, z, j)},
-            )
-            cp.start()
-            direct.append(cp)
+            {"group": (y + dy) % NY},
+        )
+        first_legs.append(cp)
+        do([], [cp], is_last(dy, x, z, c))
+
+    def rows_to(*ways):
+        for dy in ways:
+            to = (y + dy) % NY
+            for j in range(NC):
+                cp = remote(
+                    send.at[to, j], recv.at[here], a_send.at[len(direct)], a_recv.at[here],
+                    {"group": to, "blk": blk_of(x, z, j)},
+                )
+                direct.append(cp)
+                do([], [cp], is_last(dy, x, z, j))
+
+    rows_to(3, 5, 2, 6)
     own = pltpu.make_async_copy(send.at[y, c], recv.at[here], own_sem)
     own.start()
-    cross = remote(send.at[y, 1 - c], recv.at[here], a_send.at[12], a_recv.at[here], partner)
-    cross.start()
 
     for k in range(1, NZ):
-        wz[k - 1].wait_recv()
-        for cp in wx[k]:
-            cp.start()
-    second_legs = []
+        late = is_last(0, x, (z + NZ - k) % NZ, c)
+        do([wz[k]], [], late)
+        do([], [wx[k][0]], late | right_last)
+        do([], [wx[k][1]], late | left_last)
     for j in range(NC):
-        first_legs[j].wait_recv()
-        source = (y + (NY - 2 if j == 0 else 2)) % NY
-        to = (y + (2 if j == 0 else NY - 2)) % NY
-        slot = source * NC + c
+        back, on = (NY - 2, 2) if j == 0 else (2, NY - 2)
+        slot = ((y + back) % NY) * NC + c
         cp = remote(
             relay.at[j], recv.at[slot], a_send.at[13 + j], a_recv.at[slot],
-            {"group": to, "blk": blk_of(x, z, j)},
-        )
-        cp.start()
+            {"group": (y + on) % NY, "blk": blk_of(x, z, j)},
+        )
         second_legs.append(cp)
+        do([first_legs[j]], [cp], is_last(back, x, z, c) | is_last(on, x, z, j))
+    rows_to(1, 7)
+    cross = remote(send.at[y, 1 - c], recv.at[here], a_send.at[12], a_recv.at[here], partner)
+    do([], [cross], is_last(0, x, z, 1 - c))
     for k in range(NZ):
         for cp, onward in zip(wx[k], wr[k]):
-            cp.wait_recv()
-            onward.start()
+            do([cp], [onward], right_last | left_last)
+
+    @pl.when(by_last)
+    def _():
+        pl.semaphore_wait(ready, 1)
+        for touches_last, act in list(later):
+            pl.when(touches_last)(act)
+
     for k in range(NZ):
         for cp in wr[k]:
             cp.wait_recv()
@@ -299,7 +320,7 @@
         total = total + z_buf[k].astype(F32)
     out_ref[...] = total.T.astype(BF)
 
-    for cp in wz + direct + first_legs + second_legs + swaps + zs + [swap_cot, cross]:
+    for cp in wz[1:] + direct + first_legs + second_legs + swaps + zs + [swap_cot, cross]:
         cp.wait_send()
     for group in wx + wr + rs:
         for cp in group:
@@ -311,15 +332,15 @@
     top, hid = act_cotangent.shape[1:]
     half = width // 2
     dma = pltpu.SemaphoreType.DMA
-    any_spec = pl.BlockSpec(memory_space=pl.ANY)
+    hbm = pl.BlockSpec(memory_space=pltpu.HBM)
     out = pl.pallas_call(
         kernel,
         out_shape=jax.ShapeDtypeStruct((rows, 2 * hid), BF),
-        in_specs=[any_spec] * 5,
+        in_specs=[hbm] * 5,
         out_specs=pl.BlockSpec(memory_space=pltpu.VMEM),
         scratch_shapes=[
             pltpu.VMEM((rows, width), BF),
-            pltpu.VMEM((rows, top), jnp.int32),
+            pltpu.VMEM((top, rows), jnp.int32),
             pltpu.VMEM((rows * top, hid), BF),
             pltpu.VMEM((rows, 1, 2, hid), BF),
             pltpu.VMEM((1, 1, 2, hid // 128), BF),
@@ -339,7 +360,7 @@
             pltpu.VMEM((NZ, 2 * hid, 128), BF),
             pltpu.VMEM((NZ, 2 * hid, 128), BF),
             pltpu.VMEM((NZ, 2 * hid, 128), BF),
-            dma((5,)), dma,
+            dma((5,)), dma, pltpu.SemaphoreType.REGULAR,
             dma((16,)), dma((16,)), dma((2,)), dma((2,)),
             dma((NZ,)), dma((NZ,)), dma((4, NZ)), dma((4, NZ)),
             dma((3,)), dma((3,)),
@@ -348,7 +369,13 @@
         compiler_params=pltpu.CompilerParams(
             collective_id=0, has_side_effects=True, vmem_limit_bytes=48 * 1024 * 1024
         ),
-    )(tokens, routed_experts, act_cotangent.reshape(rows * top, hid), weight_codes, weight_scales)
+    )(*[
+        pltpu.with_memory_space_constraint(a, pltpu.HBM)
+        for a in (
+            tokens, routed_experts.T, act_cotangent.reshape(rows * top, hid),
+            weight_codes, weight_scales,
+        )
+    ])
     return out.reshape(rows, 1, 2, hid)
 
 

time: 70.5 us -> 73 us (1.035)
  Pallas kernels: 65.6 us -> 72.2 us
  local copies, waits for them, and re-layouts: 4.66 us -> 0.69 us
    pallas_call x1, Pallas kernels: 65.6 us -> 72.2 us  [local(): pl.pallas_call(kernel, out_shape=jax.ShapeDtypeStruct((rows, 2 * hid), BF...]
    unnamed x9 -> x0, local copies, waits for them, and re-layouts: 3.97 us -> none
where the time goes in v2:
time: 73 us; the launch traced here: 72.9 us
  Pallas kernels  72.2 us (99%)
    pallas_call x1, Pallas kernels, local(): pl.pallas_call(kernel, out_shape=jax.ShapeDtypeStruct((rows, 2 * hid), BF...  72.2 us

profile of v2, /device:TPU:1, one launch (start us, length us, event | category | flops | bytes accessed | tf_op | source)
XLA Modules:
  0.0 72.9 jit_solution(11932608902471436385)
XLA Ops:
  0.0 72.2 %shard_map.55 = bf16[128,512]{1,0:T(8,128)(2,1)S(1)} custom-call(bf16[128,4096]{1,0:T(8,128)(2,1)} %tokens_hbm.1, s32[8,128]{1,0:T(8,128)} %bitcast.4, bf16[1024,256]{1,0:T(8,128)(2,1)} %bitcast.3, bf16[128,1,2,256]{3,2,1,0:T(2,128)(2,1)} %codes_hbm.1, bf16[1,1,2,2]{3,2,1,0:T(2,128)(2,1)} %scales_hbm.1), custom_call_target="tpu_custom_call" | custom-call | tf_op jit(solution)/shard_map/pallas_call | solution.py:336
  72.2 0.7 reshape.7

commit v3 on v2

--- a/solution.py
+++ b/solution.py
@@ -36,6 +36,7 @@
         return xx * (NZ * NC) + zz * NC + cc
 
     right, left, across = (x + 1) % NX, (x + NX - 1) % NX, (x + 2) % NX
+    z_near = [z, z + 1 - 2 * (z % 2), 2 - z // 2, 3 - 3 * (z // 2)]
     to_right = {"blk": blk_of(right, z, c)}
     to_left = {"blk": blk_of(left, z, c)}
     partner = {"blk": blk_of(x, z, 1 - c)}
@@ -61,12 +62,12 @@
     peers += [(0, x, (z + k) % NZ, c) for k in range(1, NZ)]
 
     def is_last(dy, xx, zz, cc):
-        return ((y + dy) % NY == 0) & (blk_of(xx, zz, cc) == 0)
+        return ((y + dy) % NY == 0) & (blk_of(xx, zz, cc) == 0) & (lax.axis_index("att") == 0)
 
     def place(dy, xx, zz, cc):
         return {"group": (y + dy) % NY, "blk": blk_of(xx, zz, cc)}
 
-    last = (y == 0) & (b == 0)
+    last = is_last(0, x, z, c)
     by_last = functools.reduce(lambda p, q: p | q, [is_last(*peer) for peer in peers])
     owed = by_last.astype(jnp.int32)
     barrier = pltpu.get_barrier_semaphore()
@@ -75,6 +76,12 @@
     def _():
         for peer in peers:
             pl.semaphore_signal(barrier, inc=1, device_id=place(*peer), device_id_type=MESH)
+
+    @pl.when(last)
+    def _():
+        pl.semaphore_wait(barrier, len(peers))
+        for peer in peers:
+            pl.semaphore_signal(ready, inc=1, device_id=place(*peer), device_id_type=MESH)
 
     loads[0].wait()
     loads[1].wait()
@@ -86,6 +93,30 @@
             piece = codes32[:, j, q * 128:(q + 1) * 128] * sc[j:j + 1, q:q + 1]
             at = q * 256 + j * 128
             w[mine_w, :, at:at + 128] = piece.astype(BF)
+
+    top, low = pl.ds(0, 64), pl.ds(64, 64)
+    wz, wx, wr = [None], [], []
+    for k in range(NZ):
+        row_of = z_near[k] * NX
+        here_w, left_w, right_w = w.at[row_of + x], w.at[row_of + left], w.at[row_of + right]
+        if k:
+            wz.append(remote(
+                w.at[mine_w], w.at[mine_w], wz_send.at[k], wz_recv.at[z],
+                {"blk": blk_of(x, z_near[k], c)},
+            ))
+        wx.append([
+            remote(here_w, here_w, wx_send.at[0, k], wx_recv.at[0, k], to_right),
+            remote(here_w, here_w, wx_send.at[1, k], wx_recv.at[1, k], to_left),
+        ])
+        wr.append([
+            remote(left_w.at[top], left_w.at[top], wx_send.at[2, k], wx_recv.at[2, k], to_right),
+            remote(right_w.at[low], right_w.at[low], wx_send.at[3, k], wx_recv.at[3, k], to_left),
+        ])
+
+    @pl.when(last)
+    def _():
+        for cp in wz[1:] + wx[0]:
+            cp.start()
 
     loads[2].wait()
     ids = routed[...].T
@@ -110,47 +141,40 @@
             cot[:, j * 128:(j + 1) * 128].astype(BF).reshape(NY, CAP, 128)
         )
 
-    pl.semaphore_wait(barrier, len(peers) - owed)
-
-    @pl.when(last)
-    def _():
-        for peer in peers:
-            pl.semaphore_signal(ready, inc=1, device_id=place(*peer), device_id_type=MESH)
-
-    later = []
-
-    def do(waits, starts, touches_last):
+    @pl.when(jnp.logical_not(last))
+    def _():
+        pl.semaphore_wait(barrier, len(peers) - owed)
+
+    later_to, later_from, no = [], [], jnp.logical_not
+
+    def do(waits, starts, to_last, from_last=None):
         def act():
             for cp in waits:
                 cp.wait_recv()
             for cp in starts:
                 cp.start()
 
-        pl.when(jnp.logical_not(touches_last))(act)
-        later.append((touches_last, act))
-
-    wz, wx, wr = [None], [], []
-    for k in range(1, NZ):
-        wz.append(remote(
-            w.at[mine_w], w.at[mine_w], wz_send.at[k], wz_recv.at[k],
-            {"blk": blk_of(x, (z + k) % NZ, c)},
-        ))
-        do([], [wz[k]], is_last(0, x, (z + k) % NZ, c))
-    top, low = pl.ds(0, 64), pl.ds(64, 64)
-    for k in range(NZ):
-        row_of = ((z + NZ - k) % NZ) * NX
-        here_w, left_w, right_w = w.at[row_of + x], w.at[row_of + left], w.at[row_of + right]
-        wx.append([
-            remote(here_w, here_w, wx_send.at[0, k], wx_recv.at[0, k], to_right),
-            remote(here_w, here_w, wx_send.at[1, k], wx_recv.at[1, k], to_left),
-        ])
-        wr.append([
-            remote(left_w.at[top], left_w.at[top], wx_send.at[2, k], wx_recv.at[2, k], to_right),
-            remote(right_w.at[low], right_w.at[low], wx_send.at[3, k], wx_recv.at[3, k], to_left),
-        ])
+        if from_last is None:
+            pl.when(no(to_last))(act)
+            later_to.append(([to_last], act))
+        elif to_last is None:
+            pl.when(no(from_last))(act)
+            later_from.append(([from_last], act))
+        else:
+            pl.when(no(to_last) & no(from_last))(act)
+            later_to.append(([to_last, no(from_last)], act))
+            later_from.append(([from_last], act))
+
     right_last, left_last = is_last(0, right, z, c), is_last(0, left, z, c)
-    do([], [wx[0][0]], right_last)
-    do([], [wx[0][1]], left_last)
+
+    near_last = [is_last(0, x, zz, c) for zz in z_near]
+
+    @pl.when(jnp.logical_not(last))
+    def _():
+        for k in range(1, NZ):
+            do([], [wz[k]], near_last[k])
+        do([], [wx[0][0]], right_last)
+        do([], [wx[0][1]], left_last)
 
     loads[3].wait()
     for pair in range(NX * NZ):
@@ -170,26 +194,36 @@
         first_legs.append(cp)
         do([], [cp], is_last(dy, x, z, c))
 
-    def rows_to(*ways):
-        for dy in ways:
-            to = (y + dy) % NY
-            for j in range(NC):
-                cp = remote(
-                    send.at[to, j], recv.at[here], a_send.at[len(direct)], a_recv.at[here],
-                    {"group": to, "blk": blk_of(x, z, j)},
-                )
-                direct.append(cp)
-                do([], [cp], is_last(dy, x, z, j))
-
-    rows_to(3, 5, 2, 6)
+    def rows_to(dy):
+        to = (y + dy) % NY
+        for j in range(NC):
+            direct.append(remote(
+                send.at[to, j], recv.at[here], a_send.at[len(direct)], a_recv.at[here],
+                {"group": to, "blk": blk_of(x, z, j)},
+            ))
+        return direct[-NC:]
+
+    for dy in (3, 5, 2, 6):
+        for j, cp in enumerate(rows_to(dy)):
+            do([], [cp], is_last(dy, x, z, j))
     own = pltpu.make_async_copy(send.at[y, c], recv.at[here], own_sem)
     own.start()
 
     for k in range(1, NZ):
-        late = is_last(0, x, (z + NZ - k) % NZ, c)
-        do([wz[k]], [], late)
-        do([], [wx[k][0]], late | right_last)
-        do([], [wx[k][1]], late | left_last)
+        late = near_last[k]
+        near_w = w.at[z_near[k] * NX + x]
+        do([remote(near_w, near_w, wz_send.at[k], wz_recv.at[z_near[k]], partner)], [], None, late)
+        do([], [wx[k][0]], right_last, late)
+        do([], [wx[k][1]], left_last, late)
+    do([wx[0][0]], [wr[0][0]], right_last, left_last)
+    do([wx[0][1]], [wr[0][1]], left_last, right_last)
+
+    @pl.when(by_last)
+    def _():
+        pl.semaphore_wait(ready, 1)
+        for flags, act in later_to + later_from:
+            pl.when(functools.reduce(lambda p, q: p & q, flags))(act)
+
     for j in range(NC):
         back, on = (NY - 2, 2) if j == 0 else (2, NY - 2)
         slot = ((y + back) % NY) * NC + c
@@ -198,20 +232,17 @@
             {"group": (y + on) % NY, "blk": blk_of(x, z, j)},
         )
         second_legs.append(cp)
-        do([first_legs[j]], [cp], is_last(back, x, z, c) | is_last(on, x, z, j))
-    rows_to(1, 7)
+        first_legs[j].wait_recv()
+        cp.start()
+    for dy in (1, 7):
+        for cp in rows_to(dy):
+            cp.start()
     cross = remote(send.at[y, 1 - c], recv.at[here], a_send.at[12], a_recv.at[here], partner)
-    do([], [cross], is_last(0, x, z, 1 - c))
-    for k in range(NZ):
+    cross.start()
+    for k in range(1, NZ):
         for cp, onward in zip(wx[k], wr[k]):
-            do([cp], [onward], right_last | left_last)
-
-    @pl.when(by_last)
-    def _():
-        pl.semaphore_wait(ready, 1)
-        for touches_last, act in list(later):
-            pl.when(touches_last)(act)
-
+            cp.wait_recv()
+            onward.start()
     for k in range(NZ):
         for cp in wr[k]:
             cp.wait_recv()
@@ -250,7 +281,7 @@
     upper, lower = pl.ds(0, hid), pl.ds(hid, hid)
 
     def z_of(k):
-        return (z + 1 + k) % NZ
+        return z_near[NZ - 1 - k]
 
     def product(k):
         zz = z_of(k)
@@ -276,15 +307,19 @@
     rs = [sends(k) for k in range(NZ)]
     zs = [
         remote(
-            g.at[z_of(k), x], z_buf.at[k], z_send.at[k], z_recv.at[k],
+            g.at[z_of(k), x], z_buf.at[z], z_send.at[k], z_recv.at[z],
             {"blk": blk_of(x, z_of(k), c)},
         )
         for k in range(NZ - 1)
     ]
 
-    def begin(k):
+    def far_start(k):
         product(k)
-        for cp in rs[k][:4]:
+        for cp in rs[k][:2]:
+            cp.start()
+
+    def near_start(k):
+        for cp in rs[k][2:4]:
             cp.start()
 
     def pass_on(k):
@@ -306,18 +341,27 @@
         g[z_of(k), x] = gathered(k).astype(BF)
         zs[k].start()
 
-    begin(0)
-    begin(1)
-    for k in range(NZ):
-        pass_on(k)
-        if k + 2 < NZ:
-            begin(k + 2)
-        if k >= 1:
-            finish(k - 1)
+    far_start(0)
+    far_start(1)
+    near_start(0)
+    near_start(1)
+    far_start(2)
+    pass_on(0)
+    near_start(2)
+    pass_on(1)
+    product(3)
+    pass_on(2)
+    finish(0)
+    for cp in rs[3][:4]:
+        cp.start()
+    finish(1)
+    finish(2)
+    pass_on(3)
     total = gathered(NZ - 1)
-    for k in range(NZ - 1):
-        zs[k].wait_recv()
-        total = total + z_buf[k].astype(F32)
+    for k in range(1, NZ):
+        got = z_buf.at[z_near[k]]
+        remote(got, got, z_send.at[k], z_recv.at[z_near[k]], partner).wait_recv()
+        total = total + got[...].astype(F32)
     out_ref[...] = total.T.astype(BF)
 
     for cp in wz[1:] + direct + first_legs + second_legs + swaps + zs + [swap_cot, cross]:

time: 73 us -> 66.3 us (0.908)
  Pallas kernels: 72.2 us -> 65.5 us
    pallas_call x1, Pallas kernels: 72.2 us -> 65.5 us  [local(): pl.pallas_call(kernel, out_shape=jax.ShapeDtypeStruct((rows, 2 * hid), BF...]
where the time goes in v3:
time: 66.3 us; the launch traced here: 66.2 us
  Pallas kernels  65.5 us (99%)
  local copies, waits for them, and re-layouts  0.69 us (1%)
    pallas_call x1, Pallas kernels, local(): pl.pallas_call(kernel, out_shape=jax.ShapeDtypeStruct((rows, 2 * hid), BF...  65.5 us

profile of v3, /device:TPU:1, one launch (start us, length us, event | category | flops | bytes accessed | tf_op | source)
XLA Modules:
  0.0 66.2 jit_solution(7935704139853975317)
XLA Ops:
  0.0 65.5 %shard_map.55 = bf16[128,512]{1,0:T(8,128)(2,1)S(1)} custom-call(bf16[128,4096]{1,0:T(8,128)(2,1)} %tokens_hbm.1, s32[8,128]{1,0:T(8,128)} %bitcast.4, bf16[1024,256]{1,0:T(8,128)(2,1)} %bitcast.3, bf16[128,1,2,256]{3,2,1,0:T(2,128)(2,1)} %codes_hbm.1, bf16[1,1,2,2]{3,2,1,0:T(2,128)(2,1)} %scales_hbm.1), custom_call_target="tpu_custom_call" | custom-call | tf_op jit(solution)/shard_map/pallas_call | solution.py:380
  65.5 0.7 %reshape.7 = bf16[128,1,2,256]{3,2,0,1:T(2,128)(2,1)} reshape(bf16[128,512]{1,0:T(8,128)(2,1)S(1)} %shard_map.55) | data formatting | bytes 262144 | tf_op jit(solution)/shard_map/reshape | solution.py:423

commit v4 on v3

--- a/solution.py
+++ b/solution.py
@@ -21,7 +21,7 @@
 def kernel(
     tokens_hbm, routed_hbm, act_hbm, codes_hbm, scales_hbm, out_ref,
     tok, routed, act, codes, scales, codes32, spread, send, recv, relay,
-    w, part, other, cot_other, p_t, g, r_a, r_b, f_l, f_r, z_buf,
+    w, part, part_sent, other, cot_other, p_t, g, r_a, r_b, f_l, f_r, z_buf,
     in_sem, own_sem, ready, a_send, a_recv, rl_send, rl_recv,
     wz_send, wz_recv, wx_send, wx_recv, ex_send, ex_recv,
     rs_send, rs_recv, z_send, z_recv,
@@ -203,46 +203,74 @@
             ))
         return direct[-NC:]
 
-    for dy in (3, 5, 2, 6):
+    for dy in (3, 5):
         for j, cp in enumerate(rows_to(dy)):
             do([], [cp], is_last(dy, x, z, j))
     own = pltpu.make_async_copy(send.at[y, c], recv.at[here], own_sem)
     own.start()
 
-    for k in range(1, NZ):
-        late = near_last[k]
+    def z_rows(k):
         near_w = w.at[z_near[k] * NX + x]
-        do([remote(near_w, near_w, wz_send.at[k], wz_recv.at[z_near[k]], partner)], [], None, late)
-        do([], [wx[k][0]], right_last, late)
-        do([], [wx[k][1]], left_last, late)
-    do([wx[0][0]], [wr[0][0]], right_last, left_last)
-    do([wx[0][1]], [wr[0][1]], left_last, right_last)
+        return remote(near_w, near_w, wz_send.at[k], wz_recv.at[z_near[k]], partner)
+
+    def pass_z(k):
+        z_rows(k).wait_recv()
+        for cp in wx[k]:
+            cp.start()
+
+    def pass_half(k):
+        for cp, onward in zip(wx[k], wr[k]):
+            cp.wait_recv()
+            onward.start()
+
+    do([z_rows(1)], [], None, near_last[1])
+    do([], [wx[1][0]], right_last, near_last[1])
+    do([], [wx[1][1]], left_last, near_last[1])
 
     @pl.when(by_last)
     def _():
         pl.semaphore_wait(ready, 1)
-        for flags, act in later_to + later_from:
+        for flags, act in later_to:
             pl.when(functools.reduce(lambda p, q: p & q, flags))(act)
 
+    held = []
     for j in range(NC):
         back, on = (NY - 2, 2) if j == 0 else (2, NY - 2)
         slot = ((y + back) % NY) * NC + c
-        cp = remote(
+        second_legs.append(remote(
             relay.at[j], recv.at[slot], a_send.at[13 + j], a_recv.at[slot],
             {"group": (y + on) % NY, "blk": blk_of(x, z, j)},
-        )
-        second_legs.append(cp)
+        ))
+        held.append(last | is_last(back, x, z, c))
+
+    def pass_rows(j):
         first_legs[j].wait_recv()
-        cp.start()
+        second_legs[j].start()
+
+    for dy in (2, 6):
+        for cp in rows_to(dy):
+            cp.start()
+    for j in range(NC):
+        pl.when(no(held[j]))(functools.partial(pass_rows, j))
     for dy in (1, 7):
         for cp in rows_to(dy):
             cp.start()
     cross = remote(send.at[y, 1 - c], recv.at[here], a_send.at[12], a_recv.at[here], partner)
     cross.start()
-    for k in range(1, NZ):
-        for cp, onward in zip(wx[k], wr[k]):
-            cp.wait_recv()
-            onward.start()
+    pass_z(2)
+    pass_half(0)
+    pass_z(3)
+
+    @pl.when(by_last)
+    def _():
+        for flags, act in later_from:
+            pl.when(functools.reduce(lambda p, q: p & q, flags))(act)
+
+    pass_half(1)
+    for j in range(NC):
+        pl.when(held[j])(functools.partial(pass_rows, j))
+    pass_half(2)
+    pass_half(3)
     for k in range(NZ):
         for cp in wr[k]:
             cp.wait_recv()
@@ -261,34 +289,35 @@
     rows_here = recv[:, :, :half].reshape(NY * NC * CAP, half)
     for q in range(hid // 128):
         part[q] = dot(rows_here, w[:, :, q * 256:(q + 1) * 256].reshape(half, 256))
-        cp = remote(part.at[q], other.at[q], ex_send.at[q], ex_recv.at[q], partner)
+        part_sent[q] = part[q].astype(BF)
+        cp = remote(part_sent.at[q], other.at[q], ex_send.at[q], ex_recv.at[q], partner)
         cp.start()
         swaps.append(cp)
-    swap_cot.wait_recv()
-    for q in range(hid // 128):
+
+    def backward(q):
         swaps[q].wait_recv()
-        gate = part[q, :, :128] + other[q, :, :128]
-        up = part[q, :, 128:] + other[q, :, 128:]
+        gate = part[q, :, :128] + other[q, :, :128].astype(F32)
+        up = part[q, :, 128:] + other[q, :, 128:].astype(F32)
         mine = recv[:, :, half:].reshape(NY * NC * CAP, 128).astype(F32)
         theirs = cot_other[...].reshape(NY * NC * CAP, 128).astype(F32)
         cotangent = jnp.where(c == q, mine, theirs)
         s = jax.nn.sigmoid(gate)
         d_gate = cotangent * up * s * (1.0 + gate * (1.0 - s))
         d_up = cotangent * gate * s
-        p_t[q * 128:(q + 1) * 128, :] = d_gate.T.astype(BF)
-        p_t[hid + q * 128:hid + (q + 1) * 128, :] = d_up.T.astype(BF)
+        p_t[q * 256:q * 256 + 128, :] = d_gate.T.astype(BF)
+        p_t[q * 256 + 128:(q + 1) * 256, :] = d_up.T.astype(BF)
 
     upper, lower = pl.ds(0, hid), pl.ds(hid, hid)
 
     def z_of(k):
         return z_near[NZ - 1 - k]
 
-    def product(k):
+    def product(k, halves=(0, 1)):
         zz = z_of(k)
         cols = recv[:, :, pl.ds(pl.multiple_of(zz * (NX * 128), 128), NX * 128)].reshape(
             NY * NC * CAP, NX * 128
         )
-        for m in range(2):
+        for m in halves:
             got = dot(p_t[m * hid:(m + 1) * hid, :], cols).astype(BF)
             for xx in range(NX):
                 g[zz, xx, m * hid:(m + 1) * hid, :] = got[:, xx * 128:(xx + 1) * 128]
@@ -341,9 +370,16 @@
         g[z_of(k), x] = gathered(k).astype(BF)
         zs[k].start()
 
-    far_start(0)
+    swap_cot.wait_recv()
+    backward(0)
+    product(0, (0,))
+    rs[0][0].start()
+    rs[0][3].start()
+    backward(1)
+    product(0, (1,))
+    rs[0][1].start()
+    rs[0][2].start()
     far_start(1)
-    near_start(0)
     near_start(1)
     far_start(2)
     pass_on(0)
@@ -362,7 +398,11 @@
         got = z_buf.at[z_near[k]]
         remote(got, got, z_send.at[k], z_recv.at[z_near[k]], partner).wait_recv()
         total = total + got[...].astype(F32)
-    out_ref[...] = total.T.astype(BF)
+    for q in range(hid // 128):
+        for j in range(2):
+            out_ref[:, j * hid + q * 128:j * hid + (q + 1) * 128] = (
+                total[q * 256 + j * 128:q * 256 + (j + 1) * 128].T.astype(BF)
+            )
 
     for cp in wz[1:] + direct + first_legs + second_legs + swaps + zs + [swap_cot, cross]:
         cp.wait_send()
@@ -395,7 +435,8 @@
             pltpu.VMEM((NC, CAP, half + 128), BF),
             pltpu.VMEM((NX * NZ, 128, 2 * hid), BF),
             pltpu.VMEM((2, NY * NC * CAP, hid), F32),
-            pltpu.VMEM((2, NY * NC * CAP, hid), F32),
+            pltpu.VMEM((2, NY * NC * CAP, hid), BF),
+            pltpu.VMEM((2, NY * NC * CAP, hid), BF),
             pltpu.VMEM((NY * NC, CAP, 128), BF),
             pltpu.VMEM((2 * hid, NY * NC * CAP), BF),
             pltpu.VMEM((NZ, NX, 2 * hid, 128), BF),

time: 66.3 us -> 62.9 us (0.949)
  Pallas kernels: 65.5 us -> 61.9 us
    pallas_call x1, Pallas kernels: 65.5 us -> 61.9 us  [local(): pl.pallas_call(kernel, out_shape=jax.ShapeDtypeStruct((rows, 2 * hid), BF...]
where the time goes in v4:
time: 62.9 us; the launch traced here: 62.6 us
  Pallas kernels  61.9 us (98%)
  local copies, waits for them, and re-layouts  0.69 us (1%)
    pallas_call x1, Pallas kernels, local(): pl.pallas_call(kernel, out_shape=jax.ShapeDtypeStruct((rows, 2 * hid), BF...  61.9 us

profile of v4, /device:TPU:1, one launch (start us, length us, event | category | flops | bytes accessed | tf_op | source)
XLA Modules:
  0.0 62.6 jit_solution(4790999161803599971)
XLA Ops:
  0.0 61.9 %shard_map.55 = bf16[128,512]{1,0:T(8,128)(2,1)S(1)} custom-call(bf16[128,4096]{1,0:T(8,128)(2,1)} %tokens_hbm.1, s32[8,128]{1,0:T(8,128)} %bitcast.4, bf16[1024,256]{1,0:T(8,128)(2,1)} %bitcast.3, bf16[128,1,2,256]{3,2,1,0:T(2,128)(2,1)} %codes_hbm.1, bf16[1,1,2,2]{3,2,1,0:T(2,128)(2,1)} %scales_hbm.1), custom_call_target="tpu_custom_call" | custom-call | tf_op jit(solution)/shard_map/pallas_call | solution.py:420
  61.9 0.7 %reshape.7 = bf16[128,1,2,256]{3,2,0,1:T(2,128)(2,1)} reshape(bf16[128,512]{1,0:T(8,128)(2,1)S(1)} %shard_map.55) | data formatting | bytes 262144 | tf_op jit(solution)/shard_map/reshape | solution.py:464

commit v5 on v4

--- a/solution.py
+++ b/solution.py
@@ -380,19 +380,18 @@
     rs[0][1].start()
     rs[0][2].start()
     far_start(1)
+    pass_on(0)
     near_start(1)
     far_start(2)
-    pass_on(0)
+    pass_on(1)
+    finish(0)
     near_start(2)
-    pass_on(1)
-    product(3)
+    far_start(3)
     pass_on(2)
-    finish(0)
-    for cp in rs[3][:4]:
-        cp.start()
+    near_start(3)
     finish(1)
+    pass_on(3)
     finish(2)
-    pass_on(3)
     total = gathered(NZ - 1)
     for k in range(1, NZ):
         got = z_buf.at[z_near[k]]

time: 62.9 us -> 62.8 us (level)
  no operation moved by 1% of the time
where the time goes in v5:
time: 62.8 us; the launch traced here: 62.6 us
  Pallas kernels  61.9 us (99%)
  local copies, waits for them, and re-layouts  0.69 us (1%)
    pallas_call x1, Pallas kernels, local(): pl.pallas_call(kernel, out_shape=jax.ShapeDtypeStruct((rows, 2 * hid), BF...  61.9 us

profile of v5, /device:TPU:1, one launch (start us, length us, event | category | flops | bytes accessed | tf_op | source)
XLA Modules:
  0.0 62.6 jit_solution(5075154689520062595)
XLA Ops:
  0.0 61.9 %shard_map.55 = bf16[128,512]{1,0:T(8,128)(2,1)S(1)} custom-call(bf16[128,4096]{1,0:T(8,128)(2,1)} %tokens_hbm.1, s32[8,128]{1,0:T(8,128)} %bitcast.4, bf16[1024,256]{1,0:T(8,128)(2,1)} %bitcast.3, bf16[128,1,2,256]{3,2,1,0:T(2,128)(2,1)} %codes_hbm.1, bf16[1,1,2,2]{3,2,1,0:T(2,128)(2,1)} %scales_hbm.1), custom_call_target="tpu_custom_call" | custom-call | tf_op jit(solution)/shard_map/pallas_call | solution.py:419
  61.9 0.7 %reshape.7 = bf16[128,1,2,256]{3,2,0,1:T(2,128)(2,1)} reshape(bf16[128,512]{1,0:T(8,128)(2,1)S(1)} %shard_map.55) | data formatting | bytes 262144 | tf_op jit(solution)/shard_map/reshape | solution.py:463

commit v6 on v5

--- a/solution.py
+++ b/solution.py
@@ -223,6 +223,13 @@
             cp.wait_recv()
             onward.start()
 
+    rest = []
+    for dy in (2, 6, 1, 7):
+        for j, cp in enumerate(rows_to(dy)):
+            flag = is_last(dy, x, z, j)
+            later_to.append(([flag], cp.start))
+            rest.append((pl.when(no(flag)), cp))
+
     do([z_rows(1)], [], None, near_last[1])
     do([], [wx[1][0]], right_last, near_last[1])
     do([], [wx[1][1]], left_last, near_last[1])
@@ -247,14 +254,12 @@
         first_legs[j].wait_recv()
         second_legs[j].start()
 
-    for dy in (2, 6):
-        for cp in rows_to(dy):
-            cp.start()
+    for unless_last, cp in rest[:4]:
+        unless_last(cp.start)
     for j in range(NC):
         pl.when(no(held[j]))(functools.partial(pass_rows, j))
-    for dy in (1, 7):
-        for cp in rows_to(dy):
-            cp.start()
+    for unless_last, cp in rest[4:]:
+        unless_last(cp.start)
     cross = remote(send.at[y, 1 - c], recv.at[here], a_send.at[12], a_recv.at[here], partner)
     cross.start()
     pass_z(2)
@@ -392,11 +397,13 @@
     finish(1)
     pass_on(3)
     finish(2)
-    total = gathered(NZ - 1)
-    for k in range(1, NZ):
+    def from_z(k):
         got = z_buf.at[z_near[k]]
         remote(got, got, z_send.at[k], z_recv.at[z_near[k]], partner).wait_recv()
-        total = total + got[...].astype(F32)
+        return got[...].astype(F32)
+
+    total = from_z(3) + gathered(NZ - 1)
+    total = total + from_z(2) + from_z(1)
     for q in range(hid // 128):
         for j in range(2):
             out_ref[:, j * hid + q * 128:j * hid + (q + 1) * 128] = (

time: 62.8 us -> 62.7 us (level)
  no operation moved by 1% of the time
where the time goes in v6:
time: 62.7 us; the launch traced here: 62.6 us
  Pallas kernels  61.9 us (99%)
  local copies, waits for them, and re-layouts  0.69 us (1%)
    pallas_call x1, Pallas kernels, local(): pl.pallas_call(kernel, out_shape=jax.ShapeDtypeStruct((rows, 2 * hid), BF...  61.9 us

profile of v6, /device:TPU:1, one launch (start us, length us, event | category | flops | bytes accessed | tf_op | source)
XLA Modules:
  0.0 62.6 jit_solution(13563444677487348438)
XLA Ops:
  0.0 61.9 %shard_map.55 = bf16[128,512]{1,0:T(8,128)(2,1)S(1)} custom-call(bf16[128,4096]{1,0:T(8,128)(2,1)} %tokens_hbm.1, s32[8,128]{1,0:T(8,128)} %bitcast.4, bf16[1024,256]{1,0:T(8,128)(2,1)} %bitcast.3, bf16[128,1,2,256]{3,2,1,0:T(2,128)(2,1)} %codes_hbm.1, bf16[1,1,2,2]{3,2,1,0:T(2,128)(2,1)} %scales_hbm.1), custom_call_target="tpu_custom_call" | custom-call | tf_op jit(solution)/shard_map/pallas_call | solution.py:426
  61.9 0.7 %reshape.7 = bf16[128,1,2,256]{3,2,0,1:T(2,128)(2,1)} reshape(bf16[128,512]{1,0:T(8,128)(2,1)S(1)} %shard_map.55) | data formatting | bytes 262144 | tf_op jit(solution)/shard_map/reshape | solution.py:470

commit v7 on v6

--- a/solution.py
+++ b/solution.py
@@ -380,11 +380,14 @@
     product(0, (0,))
     rs[0][0].start()
     rs[0][3].start()
+    product(1, (0,))
+    rs[1][0].start()
     backward(1)
     product(0, (1,))
     rs[0][1].start()
     rs[0][2].start()
-    far_start(1)
+    product(1, (1,))
+    rs[1][1].start()
     pass_on(0)
     near_start(1)
     far_start(2)

time: 62.7 us -> 62.7 us (level)
  no operation moved by 1% of the time
where the time goes in v7:
time: 62.7 us; the launch traced here: 62.6 us
  Pallas kernels  61.9 us (99%)
  local copies, waits for them, and re-layouts  0.69 us (1%)
    pallas_call x1, Pallas kernels, local(): pl.pallas_call(kernel, out_shape=jax.ShapeDtypeStruct((rows, 2 * hid), BF...  61.9 us

profile of v7, /device:TPU:1, one launch (start us, length us, event | category | flops | bytes accessed | tf_op | source)
XLA Modules:
  0.0 62.6 jit_solution(5657313687238252118)
XLA Ops:
  0.0 61.9 %shard_map.55 = bf16[128,512]{1,0:T(8,128)(2,1)S(1)} custom-call(bf16[128,4096]{1,0:T(8,128)(2,1)} %tokens_hbm.1, s32[8,128]{1,0:T(8,128)} %bitcast.4, bf16[1024,256]{1,0:T(8,128)(2,1)} %bitcast.3, bf16[128,1,2,256]{3,2,1,0:T(2,128)(2,1)} %codes_hbm.1, bf16[1,1,2,2]{3,2,1,0:T(2,128)(2,1)} %scales_hbm.1), custom_call_target="tpu_custom_call" | custom-call | tf_op jit(solution)/shard_map/pallas_call | solution.py:429
  61.9 0.7 %reshape.7 = bf16[128,1,2,256]{3,2,0,1:T(2,128)(2,1)} reshape(bf16[128,512]{1,0:T(8,128)(2,1)S(1)} %shard_map.55) | data formatting | bytes 262144 | tf_op jit(solution)/shard_map/reshape | solution.py:473
